TPU v7x, 256 devices: a whole 4x4x8 slice. The times are simulated.
256 devices in a mesh: space: 16 (over x, y_lo, core), tm: 16 (over z, y_hi).
Axes of the slice: x: 4, y: 4 (y_hi: 2, y_lo: 2; y = y_hi * 2 + y_lo), z: 8, core: 2. Of those that a mesh axis runs over, the one named last changes fastest.
Arguments:
- velocity: bfloat16 [8192, 32768], P('space', 'tm'), may hold values from -6 to 6
- pressure_modes: bfloat16 [32768, 1024], P('tm'), may hold values from -6 to 6
- partner: int32 [8192], P('space'), may hold values from 0 to 8191, as said below
- counts: int32 [16], P('tm'), may hold values from 2048 to 31744, as said below
Outputs:
- residual: bfloat16 [8192, 32768], P('space', 'tm')
Inputs may be any that keep to these rules, and one draw needn't show every extreme that they name: partner pairs each row of the rows of space index s with a row of space index s + 8 or s - 8, one to one, and partner[partner[r]] = r. counts[j] lies between max(j, 1) * 2048 and max(j, 1) * 2048 + 2048 / 2.
All inputs are finite; a program needn't handle non-finite values.
Results may differ from a plain program's by a relative error of at most 0.0034.
Values may be sent and summed in bfloat16 or wider, within the bound.
A program may use at most 64 MiB of HBM per device.

v0:
```python
import jax
import jax.numpy as jnp
from jax import lax
from jax.sharding import PartitionSpec as P


def partner_2(block, axis, distance):
    count = lax.axis_size(axis)
    route = []
    for low in range(count):
        high = low | 1 << distance
        if high != low and high < count:
            route += [(low, high), (high, low)]
    return lax.ppermute(block, axis, route)


def entering(value, axis, join, neutral):
    count, mine = (lax.axis_size(axis), lax.axis_index(axis))
    pieces = lax.all_gather(value, axis)
    total = jnp.full_like(value, 0) + jnp.asarray(neutral, value.dtype)

    def lap(position, total):
        longer = join(total, pieces[position])
        return jnp.where(position < mine, longer, total)

    return lax.fori_loop(0, count - 1, lap, total)


def add_terms(earlier, later):
    return earlier + later


def on_device(velocity, pressure_modes, partner, counts):
    shards = lax.axis_size("space")
    top_bit = shards.bit_length() - 2
    is_lower = lax.axis_index("space") < shards // 2
    rows_here = velocity.shape[0]
    half_modes = pressure_modes.shape[1] // 2
    local_index = partner % rows_here
    flip_sign = jnp.where(is_lower, 1.0, -1.0).astype(jnp.float32)
    contract = (((1,), (1,)), ((), ()))
    own_start = jnp.where(is_lower, 0, half_modes).astype(jnp.int32)
    mode_block = lax.dynamic_slice_in_dim(pressure_modes, own_start, half_modes, 1)
    own_rows = velocity.astype(jnp.float32)
    mine = jnp.dot(velocity, mode_block, preferred_element_type=jnp.float32)
    mirror_block = partner_2(velocity, "space", top_bit)
    partner_block = jnp.take(mirror_block, local_index, axis=0)
    theirs = jnp.dot(partner_block, mode_block, preferred_element_type=jnp.float32)
    correlation = 0.5 * (theirs + flip_sign * mine)
    prior_sum = entering(correlation, "tm", add_terms, jnp.zeros_like(correlation))
    scaled = (prior_sum / counts[0].astype(jnp.float32)).astype(jnp.bfloat16)
    own_pred = lax.dot_general(
        scaled, mode_block, contract, preferred_element_type=jnp.float32
    ).astype(jnp.bfloat16)
    mirror_pred = partner_2(own_pred, "space", top_bit)
    partner_pred = jnp.take(mirror_pred, local_index, axis=0)
    combined = partner_pred.astype(jnp.float32) + flip_sign * own_pred.astype(jnp.float32)
    return (own_rows - combined).astype(jnp.bfloat16)


def solution(mesh):
    placed = (P("space", "tm"), P("tm", None), P("space"), P("tm"))
    return jax.shard_map(
        on_device, mesh=mesh, in_specs=placed, out_specs=P("space", "tm"), check_vma=False
    )
```

profile of v0, /device:TPU:2, one launch (start us, length us, event | category | flops | bytes accessed | tf_op | source)
XLA Modules:
  0.0 383.8 jit_solution(9236298820615070728)
XLA Ops:
  6.5 0.0 all-gather.3.cloned.1.call-start
  6.5 2.1 collective-permute-start
  8.7 0.7 compare_and_fusion
  9.4 3.5 fusion.10
  12.8 42.8 %collective-permute-done = bf16[512,2048]{1,0:T(8,128)(2,1)S(1)} collective-permute-done((bf16[512,2048]{1,0:T(8,128)(2,1)}, bf16[512,2048]{1,0:T(8,128)(2,1)S(1)}, u32[]{:S(2)}, u32[]{:S(2)}) %collective-permute-start) | collective-permute-done | bytes 2097184 | tf_op jit(solution)/shard_map/ppermute | solution.py:14
  55.6 3.3 gather_fusion
  58.9 4.5 %fusion.18 = f32[512,512]{1,0:T(8,128)} fusion(f32[512,512]{1,0:T(8,128)S(1)} %fusion.10, bf16[2048,1024]{1,0:T(8,128)(2,1)} %param.9, s32[]{:T(128)S(6)} %select_n.45, bf16[512,2048]{1,0:T(8,128)(2,1)} %gather_fusion, pred[512]{0:T(512)(128)(4,1)S(1)} %get-tuple-element.109), kind=kOutput, calls=%fused_computation.15 | convolution fusion | flops 1075314688 | bytes 6291972 | tf_op jit(solution)/shard_map/dot_general | solution.py:48
  63.4 0.0 all-gather.3.cloned.1.call-update
  64.1 227.0 %all-gather.3.cloned.1.call-done = f32[8192,512]{1,0:T(8,128)} async-done(((f32[512,512]{1,0:T(8,128)}), f32[8192,512]{1,0:T(8,128)}) %all-gather.3.cloned.1.call-update) | async-done | bytes 16777232 | tf_op jit(solution)/shard_map/all_gather | solution.py:19
  291.1 24.2 %while.14 = (s32[]{:T(128)}, f32[512,512]{1,0:T(8,128)S(1)}, s32[]{:T(128)}, f32[16,512,512]{2,1,0:T(8,128)}, s32[]{:T(128)}, /*index=5*/s32[]{:T(128)}) while((s32[]{:T(128)}, f32[512,512]{1,0:T(8,128)S(1)}, s32[]{:T(128)}, f32[16,512,512]{2,1,0:T(8,128)}, s32[]{:T(128)}, /*index=5*/s32[]{:T(128)}) %tuple.39), condition=%wide.region_1.3_spmd.clone, body=%wide.region_0.2_spmd.clone.sunk | while | flops 786436 | bytes 3145821 | solution.py:26
  291.1 1.6 add_select_fusion.3
  292.7 1.6 add_select_fusion.3
  294.3 1.6 add_select_fusion.3
  295.9 1.6 add_select_fusion.3
  297.5 1.6 add_select_fusion.3
  299.1 1.6 add_select_fusion.3
  300.8 1.6 add_select_fusion.3
  302.4 1.6 add_select_fusion.3
  304.0 1.6 add_select_fusion.3
  305.6 1.6 add_select_fusion.3
  307.2 1.6 add_select_fusion.3
  308.8 1.6 add_select_fusion.3
  310.5 1.6 add_select_fusion.3
  312.1 1.6 add_select_fusion.3
  313.7 1.6 add_select_fusion.3
  315.3 2.9 convolution_convert_fusion
  318.2 0.0 copy-start
  318.2 1.3 copy-done
  319.5 2.1 collective-permute-start.1
  321.6 46.1 %collective-permute-done.1 = bf16[512,2048]{1,0:T(8,128)(2,1)S(1)} collective-permute-done((bf16[512,2048]{1,0:T(8,128)(2,1)S(1)}, bf16[512,2048]{1,0:T(8,128)(2,1)S(1)}, u32[]{:S(2)}, u32[]{:S(2)}) %collective-permute-start.1) | collective-permute-done | bytes 2097184 | tf_op jit(solution)/shard_map/ppermute | solution.py:14
  367.7 3.3 gather_fusion.1
  371.0 5.9 %subtract_convert_fusion = bf16[512,2048]{1,0:T(8,128)(2,1)} fusion(bf16[512,2048]{1,0:T(8,128)(2,1)} %copy-done, bf16[512,2048]{1,0:T(8,128)(2,1)} %param.8, bf16[512,2048]{1,0:T(8,128)(2,1)} %gather_fusion.1, f32[]{:T(128)S(6)} %select_n.46, pred[512]{0:T(512)(128)(4,1)S(1)} %get-tuple-element.109), kind=kLoop, calls=%fused_computation.3 | loop fusion | flops 8388608 | bytes 8389124 | tf_op jit(solution)/shard_map/convert_element_type | solution.py:58
  (2 shorter events, 0.0 us)
Async XLA Ops:
  6.5 284.5 %all-gather.3.cloned.1.call-start = ((), (), s32[]{:S(2)}) async-start(), calls=%async_computation | async-start | bytes 17825792 | tf_op jit(solution)/shard_map/all_gather | solution.py:19
  6.5 49.1 %collective-permute-start = (bf16[512,2048]{1,0:T(8,128)(2,1)}, bf16[512,2048]{1,0:T(8,128)(2,1)S(1)}, u32[]{:S(2)}, u32[]{:S(2)}) collective-permute-start(bf16[512,2048]{1,0:T(8,128)(2,1)} %param.8), channel_id=1, source_target_pairs={{0,128},{128,0},{16,144},{144,16},{32,160},{160,32},{48,176},{176,... | collective-permute-start | bytes 6291464 | tf_op jit(solution)/shard_map/ppermute | solution.py:14
  318.2 1.3 copy-start
  319.5 48.1 %collective-permute-start.1 = (bf16[512,2048]{1,0:T(8,128)(2,1)S(1)}, bf16[512,2048]{1,0:T(8,128)(2,1)S(1)}, u32[]{:S(2)}, u32[]{:S(2)}) collective-permute-start(bf16[512,2048]{1,0:T(8,128)(2,1)S(1)} %convolution_convert_fusion), channel_id=1, source_target_pairs={{0,128},{128,0},{16,144},{144,16},{32,160},{160,32},{48,176},{176,... | collective-permute-start | bytes 6291464 | tf_op jit(solution)/shard_map/ppermute | solution.py:14
Sparse Core Ops, SparseCore 0:
  63.5 227.4 all-gather.2
where the time goes:
time: 385 us; the launch traced here: 384 us
  waiting for transfers between devices  316 us (82%)
  other arithmetic  30.5 us (8%)
  between operations  14.1 us (4%)
  matrix products  10.8 us (3%)
  local copies, waits for them, and re-layouts  7.93 us (2%)
  starting transfers between devices  4.2 us (1%)
    all_gather x1, waiting for transfers between devices, entering(): pieces = lax.all_gather(value, axis)  227 us
    ppermute x2, waiting for transfers between devices, partner_2(): return lax.ppermute(block, axis, route)  88.8 us
    select_n x15, other arithmetic, lap(): return jnp.where(position < mine, longer, total)  23.9 us
  transfers between devices with their start and end apart: 3, of which 3 were waited for; matrix products, arithmetic and copies ran while one was open for 1% of the time, Pallas kernels for 0%

commit v1 on v0

v1 whole, which is shorter than its diff:
```python
import functools

import jax
import jax.numpy as jnp
from jax import lax
from jax.experimental import pallas as pl
from jax.experimental.pallas import tpu as pltpu
from jax.sharding import PartitionSpec as P

MESH = pl.DeviceIdType.MESH
F32, BF16 = jnp.float32, jnp.bfloat16
CHUNKS = 4
TILE = 256
CONTRACT_LAST = (((1,), (1,)), ((), ()))


def kernel(
    shards, steps, velocity, modes, partner, counts, out,
    v, g_own, g_oth, total, mine, x1_src, x1_dst, corr, gathered, prefix, prior, x2_dst, mate,
    perm, load_sem, x1_send, x1_recv, x2_send, x2_recv, a_send, a_recv, b_send, b_recv,
):
    me, now = lax.axis_index("space"), lax.axis_index("tm")
    rows, times = v.shape
    half = g_own.shape[1]
    width = half // CHUNKS
    slab = rows // steps
    lower = me < shards // 2
    mirror = {"space": lax.rem(me + shards // 2, shards)}
    own_at = pl.multiple_of(jnp.where(lower, 0, half), half)
    oth_at = pl.multiple_of(jnp.where(lower, half, 0), half)

    def peer(d):
        return lax.rem(now + d, steps)

    loads = [
        pltpu.make_async_copy(velocity, v, load_sem.at[0]),
        pltpu.make_async_copy(modes.at[:, pl.ds(oth_at, half)], g_oth, load_sem.at[1]),
        pltpu.make_async_copy(modes.at[:, pl.ds(own_at, half)], g_own, load_sem.at[2]),
    ]
    for load in loads:
        load.start()

    barrier = pltpu.get_barrier_semaphore()
    pl.semaphore_signal(barrier, inc=1, device_id=mirror, device_id_type=MESH)
    for d in range(1, steps):
        pl.semaphore_signal(barrier, inc=1, device_id={"tm": peer(d)}, device_id_type=MESH)

    places = lax.broadcasted_iota(jnp.int32, (rows, rows), 0)
    hit = jnp.where((partner[...] & (rows - 1)) == places, 1.0, 0.0).astype(F32)
    perm[...] = hit.T.astype(BF16)
    sign = jnp.where(lower, 1.0, -1.0).astype(F32)

    loads[0].wait()
    loads[1].wait()
    x1, x2 = [], []
    for k in range(CHUNKS):
        cols = pl.ds(k * width, width)
        x1_src[k] = jnp.dot(v[...], g_oth[:, cols], preferred_element_type=F32).astype(BF16)
        if k == 0:
            pl.semaphore_wait(barrier, steps)
        copy = pltpu.make_async_remote_copy(
            src_ref=x1_src.at[k], dst_ref=x1_dst.at[k], send_sem=x1_send.at[k],
            recv_sem=x1_recv.at[k], device_id=mirror, device_id_type=MESH,
        )
        copy.start()
        x1.append(copy)
    loads[2].wait()
    mine[...] = jnp.dot(v[...], g_own[...], preferred_element_type=F32)

    def to_owner(k, d):
        owner = peer(d)
        return pltpu.make_async_remote_copy(
            src_ref=corr.at[k, pl.ds(owner * slab, slab)], dst_ref=gathered.at[k, now],
            send_sem=a_send.at[k, d - 1], recv_sem=a_recv.at[k, d - 1],
            device_id={"tm": owner}, device_id_type=MESH,
        )

    def from_owner(k, d):
        target = peer(d)
        return pltpu.make_async_remote_copy(
            src_ref=prefix.at[k, target],
            dst_ref=prior.at[pl.ds(now * slab, slab), pl.ds(k * width, width)],
            send_sem=b_send.at[k, d - 1], recv_sem=b_recv.at[k, d - 1],
            device_id={"tm": target}, device_id_type=MESH,
        )

    for k in range(CHUNKS):
        x1[k].wait_recv()
        theirs = jnp.dot(perm[...], x1_dst[k], preferred_element_type=F32)
        corr[k] = (mine[:, k * width : (k + 1) * width] + sign * theirs).astype(BF16)

        @pl.loop(1, steps)
        def _(d):
            to_owner(k, d).start()

    for k in range(CHUNKS):
        own_rows = pl.ds(now * slab, slab)
        gathered[k, now] = corr[k, own_rows]

        @pl.loop(1, steps)
        def _(d):
            to_owner(k, d).wait_recv()

        running = jnp.zeros((slab, width), F32)
        for j in range(steps):
            prefix[k, j] = running.astype(BF16)
            if j < steps - 1:
                running = running + gathered[k, j].astype(F32)
        prior[own_rows, k * width : (k + 1) * width] = prefix[k, now]

        @pl.loop(1, steps)
        def _(d):
            from_owner(k, d).start()

    for k in range(CHUNKS):

        @pl.loop(1, steps)
        def _(d):
            from_owner(k, d).wait_recv()

        copy = pltpu.make_async_remote_copy(
            src_ref=prior.at[:, pl.ds(k * width, width)], dst_ref=x2_dst.at[k],
            send_sem=x2_send.at[k], recv_sem=x2_recv.at[k], device_id=mirror, device_id_type=MESH,
        )
        copy.start()
        x2.append(copy)

    @pl.loop(0, times // TILE)
    def _(i):
        at = pl.ds(pl.multiple_of(i * TILE, TILE), TILE)
        total[:, at] = lax.dot_general(
            prior[...], g_own[at, :], CONTRACT_LAST, preferred_element_type=F32
        )

    for k in range(CHUNKS):
        x2[k].wait_recv()
        turned = jnp.dot(perm[...], x2_dst[k], preferred_element_type=F32)
        mate[:, k * width : (k + 1) * width] = (-sign * turned).astype(BF16)

    scale = 0.5 / counts[0].astype(F32)

    @pl.loop(0, times // TILE)
    def _(i):
        at = pl.ds(pl.multiple_of(i * TILE, TILE), TILE)
        mirrored = lax.dot_general(
            mate[...], g_oth[at, :], CONTRACT_LAST, preferred_element_type=F32
        )
        combined = (total[:, at] + mirrored) * scale
        out[:, at] = (v[:, at].astype(F32) - combined).astype(out.dtype)

    for k in range(CHUNKS):
        x1[k].wait_send()
        x2[k].wait_send()

        @pl.loop(1, steps)
        def _(d):
            to_owner(k, d).wait_send()
            from_owner(k, d).wait_send()


def solution(mesh):
    shards, steps = mesh.shape["space"], mesh.shape["tm"]

    def on_device(velocity, pressure_modes, partner, counts):
        rows, times = velocity.shape
        half = pressure_modes.shape[1] // 2
        width = half // CHUNKS
        slab = rows // steps
        dma = pltpu.SemaphoreType.DMA
        return pl.pallas_call(
            functools.partial(kernel, shards, steps),
            out_shape=jax.ShapeDtypeStruct((rows, times), BF16),
            in_specs=[
                pl.BlockSpec(memory_space=pl.ANY),
                pl.BlockSpec(memory_space=pl.ANY),
                pl.BlockSpec(memory_space=pltpu.VMEM),
                pl.BlockSpec(memory_space=pltpu.SMEM),
            ],
            out_specs=pl.BlockSpec(memory_space=pltpu.VMEM),
            scratch_shapes=[
                pltpu.VMEM((rows, times), BF16),
                pltpu.VMEM((times, half), BF16),
                pltpu.VMEM((times, half), BF16),
                pltpu.VMEM((rows, times), F32),
                pltpu.VMEM((rows, half), F32),
                pltpu.VMEM((CHUNKS, rows, width), BF16),
                pltpu.VMEM((CHUNKS, rows, width), BF16),
                pltpu.VMEM((CHUNKS, rows, width), BF16),
                pltpu.VMEM((CHUNKS, steps, slab, width), BF16),
                pltpu.VMEM((CHUNKS, steps, slab, width), BF16),
                pltpu.VMEM((rows, half), BF16),
                pltpu.VMEM((CHUNKS, rows, width), BF16),
                pltpu.VMEM((rows, half), BF16),
                pltpu.VMEM((rows, rows), BF16),
                dma((3,)),
                dma((CHUNKS,)), dma((CHUNKS,)), dma((CHUNKS,)), dma((CHUNKS,)),
                dma((CHUNKS, steps - 1)), dma((CHUNKS, steps - 1)),
                dma((CHUNKS, steps - 1)), dma((CHUNKS, steps - 1)),
            ],
            compiler_params=pltpu.CompilerParams(
                collective_id=0, has_side_effects=True, vmem_limit_bytes=48 << 20
            ),
        )(velocity, pressure_modes, partner.reshape(1, rows), counts)

    placed = (P("space", "tm"), P("tm", None), P("space"), P("tm"))
    return jax.shard_map(
        on_device, mesh=mesh, in_specs=placed, out_specs=P("space", "tm"), check_vma=False
    )
```

time: 385 us -> 57.6 us (0.15)
  waiting for transfers between devices: 316 us -> 0 us
  Pallas kernels: 0 us -> 52.9 us
  other arithmetic: 30.5 us -> 0 us
  between operations: 14.1 us -> 0.67 us
  matrix products: 10.8 us -> 0 us
  local copies, waits for them, and re-layouts: 7.93 us -> 3.59 us
  starting transfers between devices: 4.2 us -> 0 us
    all_gather x1 -> x0, waiting for transfers between devices: 227 us -> none  [entering(): pieces = lax.all_gather(value, axis)]
    ppermute x2 -> x0, waiting for transfers between devices: 88.8 us -> none  [partner_2(): return lax.ppermute(block, axis, route)]
    pallas_call x0 -> x1, Pallas kernels: none -> 52.9 us  [on_device(): pl.pallas_call(functools.partial(kernel, shards, steps), out_shape=jax.Sh...]
    select_n x15 -> x0, other arithmetic: 23.9 us -> none  [lap(): return jnp.where(position < mine, longer, total)]
    dot_general x3 -> x0, matrix products: 10.8 us -> none  [the longest x1 4.48 us: on_device(): jnp.dot(partner_block, mode_block, preferred_element_type=jnp.float32)]
    gather x2 -> x0, local copies, waits for them, and re-layouts: 6.61 us -> none  [the longest x1 3.34 us: on_device(): partner_pred = jnp.take(mirror_pred, local_index, axis=0)]
    convert_element_type x1 -> x0, other arithmetic: 5.94 us -> none  [on_device(): return (own_rows - combined).astype(jnp.bfloat16)]
    ppermute x2 -> x0, starting transfers between devices: 4.2 us -> none  [partner_2(): return lax.ppermute(block, axis, route)]
  transfers between devices with their start and end apart: 3 -> 0, of which waited for: 3 -> 0; matrix products, arithmetic and copies ran while one was open for 1% -> 0% of each run, Pallas kernels for 0% -> 0%
where the time goes in v1:
time: 57.6 us; the launch traced here: 57.1 us
  Pallas kernels  52.9 us (92%)
  local copies, waits for them, and re-layouts  3.59 us (6%)
  between operations  0.67 us (1%)
    pallas_call x1, Pallas kernels, on_device(): pl.pallas_call(functools.partial(kernel, shards, steps), out_shape=jax.Sh...  52.9 us
    unnamed x5, local copies, waits for them, and re-layouts  3.59 us

profile of v1, /device:TPU:2, one launch (start us, length us, event | category | flops | bytes accessed | tf_op | source)
XLA Modules:
  0.0 57.1 jit_solution(10652216529145140286)
XLA Ops:
  0.7 0.0 copy-start
  0.7 1.6 %copy-done = bf16[512,2048]{1,0:T(8,128)(2,1)S(1)} copy-done((bf16[512,2048]{1,0:T(8,128)(2,1)S(1)}, bf16[512,2048]{1,0:T(8,128)(2,1)}, u32[]{:S(2)}) %copy-start) | copy-done | bytes 2097176
  2.2 0.0 copy-start.1
  2.2 0.7 %copy-done.1 = s32[512]{0:T(512)S(1)} copy-done((s32[512]{0:T(512)S(1)}, s32[512]{0:T(512)}, u32[]{:S(2)}) %copy-start.1) | copy-done | bytes 2072
  2.9 52.9 %shard_map.46 = bf16[512,2048]{1,0:T(8,128)(2,1)S(1)} custom-call(bf16[512,2048]{1,0:T(8,128)(2,1)S(1)} %copy-done, bf16[2048,1024]{1,0:T(8,128)(2,1)} %modes.1, s32[1,512]{1,0:T(1,128)S(1)} %bitcast.1, s32[1]{0:T(128)S(6)} %copy.6.counts), custom_call_target="tpu_custom_call" | custom-call | tf_op jit(solution)/shard_map/pallas_call | solution.py:170
  55.8 1.3 %copy.7 = bf16[512,2048]{1,0:T(8,128)(2,1)} copy(bf16[512,2048]{1,0:T(8,128)(2,1)S(1)} %shard_map.46) | data formatting | bytes 4194304
Async XLA Ops:
  0.7 1.6 %copy-start = (bf16[512,2048]{1,0:T(8,128)(2,1)S(1)}, bf16[512,2048]{1,0:T(8,128)(2,1)}, u32[]{:S(2)}) copy-start(bf16[512,2048]{1,0:T(8,128)(2,1)} %velocity.1) | copy-start | bytes 6291460
  2.2 0.7 %copy-start.1 = (s32[512]{0:T(512)S(1)}, s32[512]{0:T(512)}, u32[]{:S(2)}) copy-start(s32[512]{0:T(512)} %param.6) | copy-start | bytes 6148

commit v2 on v0

v2 whole, which is shorter than its diff:
```python
import functools

import jax
import jax.numpy as jnp
from jax import lax
from jax.experimental import pallas as pl
from jax.experimental.pallas import tpu as pltpu
from jax.sharding import PartitionSpec as P

MESH = pl.DeviceIdType.MESH
F32, BF16 = jnp.float32, jnp.bfloat16
CHUNKS = 4
TILE = 256
CONTRACT_LAST = (((1,), (1,)), ((), ()))


def kernel(
    shards, steps, velocity, modes, partner, counts, out,
    v, g_own, g_oth, pairs, total, mine, cross_src, side_src, cross_in, diag_in, side_in,
    first, pair_sum, gathered, prefix, prior, side_prior, mate_in, turned, hit, hit_t,
    load_sem, p1_send, p1_recv, a_send, a_recv, b_send, b_recv, p2_send, p2_recv,
):
    me, now = lax.axis_index("space"), lax.axis_index("tm")
    rows, times = v.shape
    half = mine.shape[1]
    part = rows // CHUNKS
    depth = steps // 2
    slab = part // depth
    z, y = now // 2, lax.rem(now, 2)
    lower = me < shards // 2
    mirror = lax.rem(me + shards // 2, shards)
    twin = now + 1 - 2 * y
    cross, side, diag = {"space": mirror}, {"tm": twin}, {"space": mirror, "tm": twin}
    own_at = jnp.where(lower, 0, 2 * half)
    oth_at = jnp.where(lower, 2 * half, 0)

    def along(d):
        return lax.rem(z + d, depth)

    def modes_at(at):
        return modes.at[:, pl.ds(pl.multiple_of(at, half), half)]

    loads = [
        pltpu.make_async_copy(partner, pairs, load_sem.at[0]),
        pltpu.make_async_copy(velocity, v, load_sem.at[1]),
        pltpu.make_async_copy(modes_at(oth_at), g_oth.at[0], load_sem.at[2]),
        pltpu.make_async_copy(modes_at(oth_at + half), g_oth.at[1], load_sem.at[3]),
        pltpu.make_async_copy(modes_at(own_at), g_own.at[0], load_sem.at[4]),
        pltpu.make_async_copy(modes_at(own_at + half), g_own.at[1], load_sem.at[5]),
    ]
    for load in loads:
        load.start()

    barrier = pltpu.get_barrier_semaphore()
    for device in (cross, side, diag):
        pl.semaphore_signal(barrier, inc=1, device_id=device, device_id_type=MESH)
    for d in range(1, depth):
        pl.semaphore_signal(
            barrier, inc=1, device_id={"tm": 2 * along(d) + y}, device_id_type=MESH
        )

    loads[0].wait()
    places = lax.broadcasted_iota(jnp.int32, (rows, rows), 0)
    found = jnp.where((pairs[...] & (rows - 1)) == places, 1.0, 0.0).astype(F32)
    hit[...] = found.astype(BF16)
    sign = jnp.where(lower, 1.0, -1.0).astype(F32)

    def send(src, dst, sems, k, device):
        return pltpu.make_async_remote_copy(
            src_ref=src, dst_ref=dst, send_sem=sems[0].at[k], recv_sem=sems[1].at[k],
            device_id=device, device_id_type=MESH,
        )

    def lines(c):
        return pl.ds(c * part, part)

    p1, p2 = (p1_send, p1_recv), (p2_send, p2_recv)
    to_cross = [
        send(cross_src.at[y, lines(c)], cross_in.at[lines(c)], p1, 3 * c, cross)
        for c in range(CHUNKS)
    ]
    to_diag = [
        send(cross_src.at[1 - y, lines(c)], diag_in.at[lines(c)], p1, 3 * c + 1, diag)
        for c in range(CHUNKS)
    ]
    to_side = [
        send(side_src.at[lines(c)], side_in.at[lines(c)], p1, 3 * c + 2, side)
        for c in range(CHUNKS)
    ]
    back_cross = [
        send(prior.at[y, lines(c)], mate_in.at[y, lines(c)], p2, 3 * c, cross)
        for c in range(CHUNKS)
    ]
    back_diag = [
        send(prior.at[1 - y, lines(c)], mate_in.at[y, lines(c)], p2, 3 * c + 1, diag)
        for c in range(CHUNKS)
    ]
    back_side = [
        send(prior.at[1 - y, lines(c)], side_prior.at[lines(c)], p2, 3 * c + 2, side)
        for c in range(CHUNKS)
    ]

    def to_owner(c, d):
        owner = along(d)
        return pltpu.make_async_remote_copy(
            src_ref=pair_sum.at[pl.ds(c * part + owner * slab, slab)],
            dst_ref=gathered.at[c, z],
            send_sem=a_send.at[c, d - 1], recv_sem=a_recv.at[c, d - 1],
            device_id={"tm": 2 * owner + y}, device_id_type=MESH,
        )

    def from_owner(c, d):
        target = along(d)
        return pltpu.make_async_remote_copy(
            src_ref=prefix.at[c, target],
            dst_ref=prior.at[0, pl.ds(c * part + z * slab, slab)],
            send_sem=b_send.at[c, d - 1], recv_sem=b_recv.at[c, d - 1],
            device_id={"tm": 2 * target + y}, device_id_type=MESH,
        )

    loads[1].wait()
    for h in range(2):
        loads[2 + h].wait()
        product = jnp.dot(v[...], g_oth[h], preferred_element_type=F32).astype(BF16)
        cross_src[h] = jnp.dot(hit[...], product, preferred_element_type=F32).astype(BF16)
    pl.semaphore_wait(barrier, depth + 2)
    for c in range(CHUNKS):
        to_cross[c].start()
        to_diag[c].start()
    loads[4].wait()
    loads[5].wait()
    side_src[...] = jnp.dot(v[...], g_own[1 - y], preferred_element_type=F32).astype(BF16)
    for c in range(CHUNKS):
        to_side[c].start()
    mine[...] = jnp.dot(v[...], g_own[y], preferred_element_type=F32)
    hit_t[...] = found.T.astype(BF16)

    def join(c):
        to_side[c].wait_recv()
        to_cross[c].wait_recv()
        to_diag[c].wait_recv()
        here = mine[lines(c)] + sign * cross_in[lines(c)].astype(F32)
        there = side_in[lines(c)].astype(F32) + sign * diag_in[lines(c)].astype(F32)
        first[lines(c)] = jnp.where(y == 0, here, there)
        pair_sum[lines(c)] = (here + there).astype(BF16)

        @pl.loop(1, depth)
        def _(d):
            to_owner(c, d).start()

    def scan(c):
        own = pl.ds(c * part + z * slab, slab)
        gathered[c, z] = pair_sum[own]

        @pl.loop(1, depth)
        def _(d):
            to_owner(c, d).wait_recv()

        running = jnp.zeros((slab, half), F32)
        for j in range(depth):
            prefix[c, j] = running.astype(BF16)
            if j < depth - 1:
                running = running + gathered[c, j].astype(F32)
        prior[0, own] = prefix[c, z]

        @pl.loop(1, depth)
        def _(d):
            from_owner(c, d).start()

    def spread(c):
        @pl.loop(1, depth)
        def _(d):
            from_owner(c, d).wait_recv()

        prior[1, lines(c)] = (prior[0, lines(c)].astype(F32) + first[lines(c)]).astype(BF16)
        back_cross[c].start()
        back_diag[c].start()
        back_side[c].start()

    for t in range(CHUNKS + 3):
        if t < CHUNKS:
            join(t)
        if 0 <= t - 1 < CHUNKS:
            scan(t - 1)
        if 0 <= t - 2 < CHUNKS:
            spread(t - 2)

    def predicted(rows_of, modes_of, i):
        at = pl.ds(pl.multiple_of(i * TILE, TILE), TILE)
        return lax.dot_general(rows_of, modes_of[at, :], CONTRACT_LAST, preferred_element_type=F32)

    for c in range(CHUNKS):
        back_side[c].wait_recv()

    @pl.loop(0, times // TILE)
    def _(i):
        at = pl.ds(pl.multiple_of(i * TILE, TILE), TILE)
        total[:, at] = predicted(prior[y], g_own.at[y], i) + predicted(
            side_prior[...], g_own.at[1 - y], i
        )

    for c in range(CHUNKS):
        back_cross[c].wait_recv()
        back_diag[c].wait_recv()
    for h in range(2):
        moved = jnp.dot(hit_t[...], mate_in[h], preferred_element_type=F32)
        turned[h] = (-sign * moved).astype(BF16)

    scale = 0.5 / counts[0].astype(F32)

    @pl.loop(0, times // TILE)
    def _(i):
        at = pl.ds(pl.multiple_of(i * TILE, TILE), TILE)
        mirrored = predicted(turned[0], g_oth.at[0], i) + predicted(turned[1], g_oth.at[1], i)
        combined = (total[:, at] + mirrored) * scale
        out[:, at] = (v[:, at].astype(F32) - combined).astype(out.dtype)

    for c in range(CHUNKS):
        for copy in (to_cross, to_diag, to_side, back_cross, back_diag, back_side):
            copy[c].wait_send()

        @pl.loop(1, depth)
        def _(d):
            to_owner(c, d).wait_send()
            from_owner(c, d).wait_send()


def solution(mesh):
    shards, steps = mesh.shape["space"], mesh.shape["tm"]

    def on_device(velocity, pressure_modes, partner, counts):
        rows, times = velocity.shape
        half = pressure_modes.shape[1] // 4
        depth = steps // 2
        slab = rows // CHUNKS // depth
        dma = pltpu.SemaphoreType.DMA
        return pl.pallas_call(
            functools.partial(kernel, shards, steps),
            out_shape=jax.ShapeDtypeStruct((rows, times), BF16),
            in_specs=[
                pl.BlockSpec(memory_space=pltpu.HBM),
                pl.BlockSpec(memory_space=pltpu.HBM),
                pl.BlockSpec(memory_space=pltpu.HBM),
                pl.BlockSpec(memory_space=pltpu.SMEM),
            ],
            out_specs=pl.BlockSpec(memory_space=pltpu.VMEM),
            scratch_shapes=[
                pltpu.VMEM((rows, times), BF16),
                pltpu.VMEM((2, times, half), BF16),
                pltpu.VMEM((2, times, half), BF16),
                pltpu.VMEM((1, rows), jnp.int32),
                pltpu.VMEM((rows, times), F32),
                pltpu.VMEM((rows, half), F32),
                pltpu.VMEM((2, rows, half), BF16),
                pltpu.VMEM((rows, half), BF16),
                pltpu.VMEM((rows, half), BF16),
                pltpu.VMEM((rows, half), BF16),
                pltpu.VMEM((rows, half), BF16),
                pltpu.VMEM((rows, half), F32),
                pltpu.VMEM((rows, half), BF16),
                pltpu.VMEM((CHUNKS, depth, slab, half), BF16),
                pltpu.VMEM((CHUNKS, depth, slab, half), BF16),
                pltpu.VMEM((2, rows, half), BF16),
                pltpu.VMEM((rows, half), BF16),
                pltpu.VMEM((2, rows, half), BF16),
                pltpu.VMEM((2, rows, half), BF16),
                pltpu.VMEM((rows, rows), BF16),
                pltpu.VMEM((rows, rows), BF16),
                dma((6,)),
                dma((3 * CHUNKS,)), dma((3 * CHUNKS,)),
                dma((CHUNKS, depth - 1)), dma((CHUNKS, depth - 1)),
                dma((CHUNKS, depth - 1)), dma((CHUNKS, depth - 1)),
                dma((3 * CHUNKS,)), dma((3 * CHUNKS,)),
            ],
            compiler_params=pltpu.CompilerParams(
                collective_id=0, has_side_effects=True, vmem_limit_bytes=48 << 20
            ),
        )(velocity, pressure_modes, partner.reshape(1, rows), counts)

    placed = (P("space", "tm"), P("tm", None), P("space"), P("tm"))
    return jax.shard_map(
        on_device, mesh=mesh, in_specs=placed, out_specs=P("space", "tm"), check_vma=False
    )
```

time: 385 us -> 53.1 us (0.14)
  waiting for transfers between devices: 316 us -> 0 us
  Pallas kernels: 0 us -> 48.1 us
  other arithmetic: 30.5 us -> 0 us
  between operations: 14.1 us -> 0.67 us
  matrix products: 10.8 us -> 0 us
  local copies, waits for them, and re-layouts: 7.93 us -> 3.59 us
  starting transfers between devices: 4.2 us -> 0 us
    all_gather x1 -> x0, waiting for transfers between devices: 227 us -> none  [entering(): pieces = lax.all_gather(value, axis)]
    ppermute x2 -> x0, waiting for transfers between devices: 88.8 us -> none  [partner_2(): return lax.ppermute(block, axis, route)]
    pallas_call x0 -> x1, Pallas kernels: none -> 48.1 us  [on_device(): pl.pallas_call(functools.partial(kernel, shards, steps), out_shape=jax.Sh...]
    select_n x15 -> x0, other arithmetic: 23.9 us -> none  [lap(): return jnp.where(position < mine, longer, total)]
    dot_general x3 -> x0, matrix products: 10.8 us -> none  [the longest x1 4.48 us: on_device(): jnp.dot(partner_block, mode_block, preferred_element_type=jnp.float32)]
    gather x2 -> x0, local copies, waits for them, and re-layouts: 6.61 us -> none  [the longest x1 3.34 us: on_device(): partner_pred = jnp.take(mirror_pred, local_index, axis=0)]
    convert_element_type x1 -> x0, other arithmetic: 5.94 us -> none  [on_device(): return (own_rows - combined).astype(jnp.bfloat16)]
    ppermute x2 -> x0, starting transfers between devices: 4.2 us -> none  [partner_2(): return lax.ppermute(block, axis, route)]
  transfers between devices with their start and end apart: 3 -> 0, of which waited for: 3 -> 0; matrix products, arithmetic and copies ran while one was open for 1% -> 0% of each run, Pallas kernels for 0% -> 0%
where the time goes in v2:
time: 53.1 us; the launch traced here: 52.4 us
  Pallas kernels  48.1 us (91%)
  local copies, waits for them, and re-layouts  3.59 us (7%)
  between operations  0.67 us (1%)
    pallas_call x1, Pallas kernels, on_device(): pl.pallas_call(functools.partial(kernel, shards, steps), out_shape=jax.Sh...  48.1 us
    unnamed x5, local copies, waits for them, and re-layouts  3.59 us

profile of v2, /device:TPU:2, one launch (start us, length us, event | category | flops | bytes accessed | tf_op | source)
XLA Modules:
  0.0 52.4 jit_solution(17074684671450901327)
XLA Ops:
  0.7 0.0 copy-start
  0.7 1.6 %copy-done = bf16[512,2048]{1,0:T(8,128)(2,1)S(1)} copy-done((bf16[512,2048]{1,0:T(8,128)(2,1)S(1)}, bf16[512,2048]{1,0:T(8,128)(2,1)}, u32[]{:S(2)}) %copy-start) | copy-done | bytes 2097176
  2.2 0.0 copy-start.1
  2.2 0.7 %copy-done.1 = s32[512]{0:T(512)S(1)} copy-done((s32[512]{0:T(512)S(1)}, s32[512]{0:T(512)}, u32[]{:S(2)}) %copy-start.1) | copy-done | bytes 2072
  2.9 48.1 %shard_map.46 = bf16[512,2048]{1,0:T(8,128)(2,1)S(1)} custom-call(bf16[512,2048]{1,0:T(8,128)(2,1)S(1)} %copy-done, bf16[2048,1024]{1,0:T(8,128)(2,1)} %modes.1, s32[1,512]{1,0:T(1,128)S(1)} %bitcast.1, s32[1]{0:T(128)S(6)} %copy.6.counts), custom_call_target="tpu_custom_call" | custom-call | tf_op jit(solution)/shard_map/pallas_call | solution.py:237
  51.1 1.3 %copy.7 = bf16[512,2048]{1,0:T(8,128)(2,1)} copy(bf16[512,2048]{1,0:T(8,128)(2,1)S(1)} %shard_map.46) | data formatting | bytes 4194304
Async XLA Ops:
  0.7 1.6 %copy-start = (bf16[512,2048]{1,0:T(8,128)(2,1)S(1)}, bf16[512,2048]{1,0:T(8,128)(2,1)}, u32[]{:S(2)}) copy-start(bf16[512,2048]{1,0:T(8,128)(2,1)} %velocity.1) | copy-start | bytes 6291460
  2.2 0.7 %copy-start.1 = (s32[512]{0:T(512)S(1)}, s32[512]{0:T(512)}, u32[]{:S(2)}) copy-start(s32[512]{0:T(512)} %param.6) | copy-start | bytes 6148

commit v3 on v2

--- a/solution.py
+++ b/solution.py
@@ -11,13 +11,17 @@
 F32, BF16 = jnp.float32, jnp.bfloat16
 CHUNKS = 4
 TILE = 256
+ORDER = (
+    (0, 0), (0, 1), (0, 2), (1, 0), (0, 3), (1, 1),
+    (1, 2), (2, 0), (1, 3), (2, 1), (2, 2), (2, 3),
+)
 CONTRACT_LAST = (((1,), (1,)), ((), ()))
 
 
 def kernel(
     shards, steps, velocity, modes, partner, counts, out,
     v, g_own, g_oth, pairs, total, mine, cross_src, side_src, cross_in, diag_in, side_in,
-    first, pair_sum, gathered, prefix, prior, side_prior, mate_in, turned, hit, hit_t,
+    g_oth_t, first, pair_sum, gathered, prefix, prior, side_prior, mate_in, turned, hit, hit_t,
     load_sem, p1_send, p1_recv, a_send, a_recv, b_send, b_recv, p2_send, p2_recv,
 ):
     me, now = lax.axis_index("space"), lax.axis_index("tm")
@@ -43,10 +47,10 @@
     loads = [
         pltpu.make_async_copy(partner, pairs, load_sem.at[0]),
         pltpu.make_async_copy(velocity, v, load_sem.at[1]),
-        pltpu.make_async_copy(modes_at(oth_at), g_oth.at[0], load_sem.at[2]),
-        pltpu.make_async_copy(modes_at(oth_at + half), g_oth.at[1], load_sem.at[3]),
-        pltpu.make_async_copy(modes_at(own_at), g_own.at[0], load_sem.at[4]),
-        pltpu.make_async_copy(modes_at(own_at + half), g_own.at[1], load_sem.at[5]),
+        pltpu.make_async_copy(modes_at(oth_at + (1 - y) * half), g_oth.at[1 - y], load_sem.at[2]),
+        pltpu.make_async_copy(modes_at(oth_at + y * half), g_oth.at[y], load_sem.at[3]),
+        pltpu.make_async_copy(modes_at(own_at + (1 - y) * half), g_own.at[1 - y], load_sem.at[4]),
+        pltpu.make_async_copy(modes_at(own_at + y * half), g_own.at[y], load_sem.at[5]),
     ]
     for load in loads:
         load.start()
@@ -119,21 +123,32 @@
         )
 
     loads[1].wait()
-    for h in range(2):
-        loads[2 + h].wait()
+    for load, h in ((loads[2], 1 - y), (loads[3], y)):
+        load.wait()
         product = jnp.dot(v[...], g_oth[h], preferred_element_type=F32).astype(BF16)
         cross_src[h] = jnp.dot(hit[...], product, preferred_element_type=F32).astype(BF16)
-    pl.semaphore_wait(barrier, depth + 2)
-    for c in range(CHUNKS):
+        if load is loads[2]:
+            pl.semaphore_wait(barrier, depth + 2)
+            to_diag[0].start()
+            to_diag[1].start()
+    to_cross[0].start()
+    to_cross[1].start()
+    for c in range(2, CHUNKS):
+        to_diag[c].start()
         to_cross[c].start()
-        to_diag[c].start()
     loads[4].wait()
-    loads[5].wait()
     side_src[...] = jnp.dot(v[...], g_own[1 - y], preferred_element_type=F32).astype(BF16)
     for c in range(CHUNKS):
         to_side[c].start()
+    loads[5].wait()
     mine[...] = jnp.dot(v[...], g_own[y], preferred_element_type=F32)
     hit_t[...] = found.T.astype(BF16)
+
+    @pl.loop(0, times // TILE)
+    def _(i):
+        at = pl.ds(pl.multiple_of(i * TILE, TILE), TILE)
+        for h in range(2):
+            g_oth_t[h, :, at] = g_oth[h, at, :].T
 
     def join(c):
         to_side[c].wait_recv()
@@ -144,16 +159,14 @@
         first[lines(c)] = jnp.where(y == 0, here, there)
         pair_sum[lines(c)] = (here + there).astype(BF16)
 
-        @pl.loop(1, depth)
-        def _(d):
+        for d in range(1, depth):
             to_owner(c, d).start()
 
     def scan(c):
         own = pl.ds(c * part + z * slab, slab)
         gathered[c, z] = pair_sum[own]
 
-        @pl.loop(1, depth)
-        def _(d):
+        for d in range(1, depth):
             to_owner(c, d).wait_recv()
 
         running = jnp.zeros((slab, half), F32)
@@ -163,55 +176,64 @@
                 running = running + gathered[c, j].astype(F32)
         prior[0, own] = prefix[c, z]
 
-        @pl.loop(1, depth)
-        def _(d):
+        for d in range(1, depth):
             from_owner(c, d).start()
 
     def spread(c):
-        @pl.loop(1, depth)
-        def _(d):
+        for d in range(1, depth):
             from_owner(c, d).wait_recv()
 
         prior[1, lines(c)] = (prior[0, lines(c)].astype(F32) + first[lines(c)]).astype(BF16)
+        back_side[c].start()
+        back_diag[c].start()
         back_cross[c].start()
-        back_diag[c].start()
-        back_side[c].start()
-
-    for t in range(CHUNKS + 3):
-        if t < CHUNKS:
-            join(t)
-        if 0 <= t - 1 < CHUNKS:
-            scan(t - 1)
-        if 0 <= t - 2 < CHUNKS:
-            spread(t - 2)
+
+    stages = [join, scan, spread]
+    for stage, c in ORDER:
+        stages[stage](c)
 
     def predicted(rows_of, modes_of, i):
         at = pl.ds(pl.multiple_of(i * TILE, TILE), TILE)
         return lax.dot_general(rows_of, modes_of[at, :], CONTRACT_LAST, preferred_element_type=F32)
 
+    def arrived(some):
+        for c in some:
+            back_diag[c].wait_recv()
+            back_cross[c].wait_recv()
+        span = slice(some[0] * part, (some[-1] + 1) * part)
+        return [
+            -sign * jnp.dot(hit_t[:, span], mate_in[h, span], preferred_element_type=F32)
+            for h in range(2)
+        ]
+
+    @pl.loop(0, times // TILE)
+    def _(i):
+        at = pl.ds(pl.multiple_of(i * TILE, TILE), TILE)
+        total[:, at] = predicted(prior[y], g_own.at[y], i)
+
+    early = arrived(range(CHUNKS // 2))
+    for h in range(2):
+        turned[h] = early[h].astype(BF16)
     for c in range(CHUNKS):
         back_side[c].wait_recv()
 
     @pl.loop(0, times // TILE)
     def _(i):
         at = pl.ds(pl.multiple_of(i * TILE, TILE), TILE)
-        total[:, at] = predicted(prior[y], g_own.at[y], i) + predicted(
-            side_prior[...], g_own.at[1 - y], i
-        )
-
-    for c in range(CHUNKS):
-        back_cross[c].wait_recv()
-        back_diag[c].wait_recv()
+        total[:, at] += predicted(side_prior[...], g_own.at[1 - y], i)
+
+    late = arrived(range(CHUNKS // 2, CHUNKS))
     for h in range(2):
-        moved = jnp.dot(hit_t[...], mate_in[h], preferred_element_type=F32)
-        turned[h] = (-sign * moved).astype(BF16)
+        turned[h] = (turned[h].astype(F32) + late[h]).astype(BF16)
 
     scale = 0.5 / counts[0].astype(F32)
 
     @pl.loop(0, times // TILE)
     def _(i):
         at = pl.ds(pl.multiple_of(i * TILE, TILE), TILE)
-        mirrored = predicted(turned[0], g_oth.at[0], i) + predicted(turned[1], g_oth.at[1], i)
+        mirrored = jnp.dot(turned[0], g_oth_t[0, :, at], preferred_element_type=F32) + jnp.dot(
+            turned[1], g_oth_t[1, :, at], preferred_element_type=F32
+        )
         combined = (total[:, at] + mirrored) * scale
         out[:, at] = (v[:, at].astype(F32) - combined).astype(out.dtype)
 
@@ -234,6 +256,10 @@
         depth = steps // 2
         slab = rows // CHUNKS // depth
         dma = pltpu.SemaphoreType.DMA
+
+        def in_hbm(array):
+            return pltpu.with_memory_space_constraint(array, pltpu.HBM)
+
         return pl.pallas_call(
             functools.partial(kernel, shards, steps),
             out_shape=jax.ShapeDtypeStruct((rows, times), BF16),
@@ -256,6 +282,7 @@
                 pltpu.VMEM((rows, half), BF16),
                 pltpu.VMEM((rows, half), BF16),
                 pltpu.VMEM((rows, half), BF16),
+                pltpu.VMEM((2, half, times), BF16),
                 pltpu.VMEM((rows, half), F32),
                 pltpu.VMEM((rows, half), BF16),
                 pltpu.VMEM((CHUNKS, depth, slab, half), BF16),
@@ -275,7 +302,7 @@
             compiler_params=pltpu.CompilerParams(
                 collective_id=0, has_side_effects=True, vmem_limit_bytes=48 << 20
             ),
-        )(velocity, pressure_modes, partner.reshape(1, rows), counts)
+        )(*map(in_hbm, (velocity, pressure_modes, partner.reshape(1, rows))), counts)
 
     placed = (P("space", "tm"), P("tm", None), P("space"), P("tm"))
     return jax.shard_map(

time: 53.1 us -> 50.9 us (0.959); the launches traced: 52.4 us -> 50.8 us
  local copies, waits for them, and re-layouts: 3.59 us -> 1.32 us
  Pallas kernels: 48.1 us -> 48.8 us
    unnamed x5 -> x1, local copies, waits for them, and re-layouts: 3.59 us -> 1.32 us
    pallas_call x1, Pallas kernels: 48.1 us -> 48.8 us  [on_device(): pl.pallas_call(functools.partial(kernel, shards, steps), out_shape=jax.Sh...]
where the time goes in v3:
time: 50.9 us; the launch traced here: 50.8 us
  Pallas kernels  48.8 us (96%)
  local copies, waits for them, and re-layouts  1.32 us (3%)
  between operations  0.66 us (1%)
    pallas_call x1, Pallas kernels, on_device(): pl.pallas_call(functools.partial(kernel, shards, steps), out_shape=jax.Sh...  48.8 us
    unnamed x1, local copies, waits for them, and re-layouts  1.32 us

profile of v3, /device:TPU:2, one launch (start us, length us, event | category | flops | bytes accessed | tf_op | source)
XLA Modules:
  0.0 50.8 jit_solution(17128907807562479283)
XLA Ops:
  0.7 48.8 %shard_map.46 = bf16[512,2048]{1,0:T(8,128)(2,1)S(1)} custom-call(bf16[512,2048]{1,0:T(8,128)(2,1)} %velocity.1, bf16[2048,1024]{1,0:T(8,128)(2,1)} %modes.1, s32[1,512]{1,0:T(1,128)} %bitcast.1, s32[1]{0:T(128)S(6)} %copy.6.counts), custom_call_target="tpu_custom_call" | custom-call | tf_op jit(solution)/shard_map/pallas_call | solution.py:263
  49.5 1.3 %copy.7 = bf16[512,2048]{1,0:T(8,128)(2,1)} copy(bf16[512,2048]{1,0:T(8,128)(2,1)S(1)} %shard_map.46) | data formatting | bytes 4194304

commit v4 on v3

--- a/solution.py
+++ b/solution.py
@@ -9,12 +9,11 @@
 
 MESH = pl.DeviceIdType.MESH
 F32, BF16 = jnp.float32, jnp.bfloat16
-CHUNKS = 4
 TILE = 256
-ORDER = (
-    (0, 0), (0, 1), (0, 2), (1, 0), (0, 3), (1, 1),
-    (1, 2), (2, 0), (1, 3), (2, 1), (2, 2), (2, 3),
-)
+PIECES = 4
+CUTS = 2
+CHUNKS = 4 * CUTS
+ORDER = sorted(((s, c) for s in range(3) for c in range(CHUNKS)), key=lambda e: e[1] + 3.9 * e[0])
 CONTRACT_LAST = (((1,), (1,)), ((), ()))
 
 
@@ -27,7 +26,7 @@
     me, now = lax.axis_index("space"), lax.axis_index("tm")
     rows, times = v.shape
     half = mine.shape[1]
-    part = rows // CHUNKS
+    part, width = rows // (CHUNKS // CUTS), half // CUTS
     depth = steps // 2
     slab = part // depth
     z, y = now // 2, lax.rem(now, 2)
@@ -46,13 +45,26 @@
 
     loads = [
         pltpu.make_async_copy(partner, pairs, load_sem.at[0]),
-        pltpu.make_async_copy(velocity, v, load_sem.at[1]),
-        pltpu.make_async_copy(modes_at(oth_at + (1 - y) * half), g_oth.at[1 - y], load_sem.at[2]),
-        pltpu.make_async_copy(modes_at(oth_at + y * half), g_oth.at[y], load_sem.at[3]),
-        pltpu.make_async_copy(modes_at(own_at + (1 - y) * half), g_own.at[1 - y], load_sem.at[4]),
-        pltpu.make_async_copy(modes_at(own_at + y * half), g_own.at[y], load_sem.at[5]),
-    ]
-    for load in loads:
+        pltpu.make_async_copy(modes_at(oth_at + y * half), g_oth.at[y], load_sem.at[1]),
+        pltpu.make_async_copy(modes_at(own_at + (1 - y) * half), g_own.at[1 - y], load_sem.at[2]),
+        pltpu.make_async_copy(modes_at(own_at + y * half), g_own.at[y], load_sem.at[3]),
+    ]
+    piece = times // PIECES
+    diag_at = pl.ds(pl.multiple_of(oth_at + (1 - y) * half, half), half)
+    pieces = []
+    for i in range(PIECES):
+        at = pl.ds(i * piece, piece)
+        pieces.append((
+            pltpu.make_async_copy(velocity.at[:, at], v.at[:, at], load_sem.at[4 + 2 * i]),
+            pltpu.make_async_copy(
+                modes.at[at, diag_at], g_oth.at[1 - y, at], load_sem.at[5 + 2 * i]
+            ),
+        ))
+    loads[0].start()
+    for pair in pieces:
+        for load in pair:
+            load.start()
+    for load in loads[1:]:
         load.start()
 
     barrier = pltpu.get_barrier_semaphore()
@@ -75,39 +87,42 @@
             device_id=device, device_id_type=MESH,
         )
 
-    def lines(c):
-        return pl.ds(c * part, part)
+    def block(c):
+        return pl.ds(c // CUTS * part, part), pl.ds(c % CUTS * width, width)
+
+    def slab_of(c, owner):
+        return pl.ds(c // CUTS * part + owner * slab, slab), pl.ds(c % CUTS * width, width)
 
     p1, p2 = (p1_send, p1_recv), (p2_send, p2_recv)
     to_cross = [
-        send(cross_src.at[y, lines(c)], cross_in.at[lines(c)], p1, 3 * c, cross)
+        send(cross_src.at[y, *block(c)], cross_in.at[*block(c)], p1, 3 * c, cross)
         for c in range(CHUNKS)
     ]
     to_diag = [
-        send(cross_src.at[1 - y, lines(c)], diag_in.at[lines(c)], p1, 3 * c + 1, diag)
+        send(cross_src.at[1 - y, *block(c)], diag_in.at[*block(c)], p1, 3 * c + 1, diag)
         for c in range(CHUNKS)
     ]
     to_side = [
-        send(side_src.at[lines(c)], side_in.at[lines(c)], p1, 3 * c + 2, side)
+        send(side_src.at[*block(c)], side_in.at[*block(c)], p1, 3 * c + 2, side)
         for c in range(CHUNKS)
     ]
     back_cross = [
-        send(prior.at[y, lines(c)], mate_in.at[y, lines(c)], p2, 3 * c, cross)
+        send(prior.at[y, *block(c)], mate_in.at[y, *block(c)], p2, 3 * c, cross)
         for c in range(CHUNKS)
     ]
     back_diag = [
-        send(prior.at[1 - y, lines(c)], mate_in.at[y, lines(c)], p2, 3 * c + 1, diag)
+        send(prior.at[1 - y, *block(c)], mate_in.at[y, *block(c)], p2, 3 * c + 1, diag)
         for c in range(CHUNKS)
     ]
     back_side = [
-        send(prior.at[1 - y, lines(c)], side_prior.at[lines(c)], p2, 3 * c + 2, side)
+        send(prior.at[1 - y, *block(c)], side_prior.at[*block(c)], p2, 3 * c + 2, side)
         for c in range(CHUNKS)
     ]
 
     def to_owner(c, d):
         owner = along(d)
         return pltpu.make_async_remote_copy(
-            src_ref=pair_sum.at[pl.ds(c * part + owner * slab, slab)],
+            src_ref=pair_sum.at[slab_of(c, owner)],
             dst_ref=gathered.at[c, z],
             send_sem=a_send.at[c, d - 1], recv_sem=a_recv.at[c, d - 1],
             device_id={"tm": 2 * owner + y}, device_id_type=MESH,
@@ -117,30 +132,36 @@
         target = along(d)
         return pltpu.make_async_remote_copy(
             src_ref=prefix.at[c, target],
-            dst_ref=prior.at[0, pl.ds(c * part + z * slab, slab)],
+            dst_ref=prior.at[0, *slab_of(c, z)],
             send_sem=b_send.at[c, d - 1], recv_sem=b_recv.at[c, d - 1],
             device_id={"tm": 2 * target + y}, device_id_type=MESH,
         )
 
+    def crossing(h, product):
+        cross_src[h] = jnp.dot(hit[...], product.astype(BF16), preferred_element_type=F32).astype(BF16)
+
+    product = jnp.zeros((rows, half), F32)
+    for i, pair in enumerate(pieces):
+        for load in pair:
+            load.wait()
+        at = pl.ds(i * piece, piece)
+        product += jnp.dot(v[:, at], g_oth[1 - y, at], preferred_element_type=F32)
+    crossing(1 - y, product)
+    pl.semaphore_wait(barrier, depth + 2)
+    for c in range(CHUNKS // 2):
+        to_diag[c].start()
     loads[1].wait()
-    for load, h in ((loads[2], 1 - y), (loads[3], y)):
-        load.wait()
-        product = jnp.dot(v[...], g_oth[h], preferred_element_type=F32).astype(BF16)
-        cross_src[h] = jnp.dot(hit[...], product, preferred_element_type=F32).astype(BF16)
-        if load is loads[2]:
-            pl.semaphore_wait(barrier, depth + 2)
-            to_diag[0].start()
-            to_diag[1].start()
-    to_cross[0].start()
-    to_cross[1].start()
-    for c in range(2, CHUNKS):
+    crossing(y, jnp.dot(v[...], g_oth[y], preferred_element_type=F32))
+    for c in range(CHUNKS // 2):
+        to_cross[c].start()
+    for c in range(CHUNKS // 2, CHUNKS):
         to_diag[c].start()
         to_cross[c].start()
-    loads[4].wait()
+    loads[2].wait()
     side_src[...] = jnp.dot(v[...], g_own[1 - y], preferred_element_type=F32).astype(BF16)
     for c in range(CHUNKS):
         to_side[c].start()
-    loads[5].wait()
+    loads[3].wait()
     mine[...] = jnp.dot(v[...], g_own[y], preferred_element_type=F32)
     hit_t[...] = found.T.astype(BF16)
 
@@ -154,27 +175,27 @@
         to_side[c].wait_recv()
         to_cross[c].wait_recv()
         to_diag[c].wait_recv()
-        here = mine[lines(c)] + sign * cross_in[lines(c)].astype(F32)
-        there = side_in[lines(c)].astype(F32) + sign * diag_in[lines(c)].astype(F32)
-        first[lines(c)] = jnp.where(y == 0, here, there)
-        pair_sum[lines(c)] = (here + there).astype(BF16)
+        here = mine[*block(c)] + sign * cross_in[*block(c)].astype(F32)
+        there = side_in[*block(c)].astype(F32) + sign * diag_in[*block(c)].astype(F32)
+        first[*block(c)] = jnp.where(y == 0, here, there)
+        pair_sum[*block(c)] = (here + there).astype(BF16)
 
         for d in range(1, depth):
             to_owner(c, d).start()
 
     def scan(c):
-        own = pl.ds(c * part + z * slab, slab)
+        own = slab_of(c, z)
         gathered[c, z] = pair_sum[own]
 
         for d in range(1, depth):
             to_owner(c, d).wait_recv()
 
-        running = jnp.zeros((slab, half), F32)
+        running = jnp.zeros((slab, width), F32)
         for j in range(depth):
             prefix[c, j] = running.astype(BF16)
             if j < depth - 1:
                 running = running + gathered[c, j].astype(F32)
-        prior[0, own] = prefix[c, z]
+        prior[0, *own] = prefix[c, z]
 
         for d in range(1, depth):
             from_owner(c, d).start()
@@ -183,7 +204,7 @@
         for d in range(1, depth):
             from_owner(c, d).wait_recv()
 
-        prior[1, lines(c)] = (prior[0, lines(c)].astype(F32) + first[lines(c)]).astype(BF16)
+        prior[1, *block(c)] = (prior[0, *block(c)].astype(F32) + first[*block(c)]).astype(BF16)
         back_side[c].start()
         back_diag[c].start()
         back_cross[c].start()
@@ -200,7 +221,7 @@
         for c in some:
             back_diag[c].wait_recv()
             back_cross[c].wait_recv()
-        span = slice(some[0] * part, (some[-1] + 1) * part)
+        span = slice(some[0] // CUTS * part, (some[-1] // CUTS + 1) * part)
         return [
             -sign * jnp.dot(hit_t[:, span], mate_in[h, span], preferred_element_type=F32)
             for h in range(2)
@@ -254,7 +275,8 @@
         rows, times = velocity.shape
         half = pressure_modes.shape[1] // 4
         depth = steps // 2
-        slab = rows // CHUNKS // depth
+        slab = rows // (CHUNKS // CUTS) // depth
+        width = half // CUTS
         dma = pltpu.SemaphoreType.DMA
 
         def in_hbm(array):
@@ -285,15 +307,15 @@
                 pltpu.VMEM((2, half, times), BF16),
                 pltpu.VMEM((rows, half), F32),
                 pltpu.VMEM((rows, half), BF16),
-                pltpu.VMEM((CHUNKS, depth, slab, half), BF16),
-                pltpu.VMEM((CHUNKS, depth, slab, half), BF16),
+                pltpu.VMEM((CHUNKS, depth, slab, width), BF16),
+                pltpu.VMEM((CHUNKS, depth, slab, width), BF16),
                 pltpu.VMEM((2, rows, half), BF16),
                 pltpu.VMEM((rows, half), BF16),
                 pltpu.VMEM((2, rows, half), BF16),
                 pltpu.VMEM((2, rows, half), BF16),
                 pltpu.VMEM((rows, rows), BF16),
                 pltpu.VMEM((rows, rows), BF16),
-                dma((6,)),
+                dma((4 + 2 * PIECES,)),
                 dma((3 * CHUNKS,)), dma((3 * CHUNKS,)),
                 dma((CHUNKS, depth - 1)), dma((CHUNKS, depth - 1)),
                 dma((CHUNKS, depth - 1)), dma((CHUNKS, depth - 1)),

time: 50.9 us -> 49.6 us (0.974); the launches traced: 50.8 us -> 48.8 us
  Pallas kernels: 48.8 us -> 46.8 us
    pallas_call x1, Pallas kernels: 48.8 us -> 46.8 us  [on_device(): pl.pallas_call(functools.partial(kernel, shards, steps), out_shape=jax.Sh...]
where the time goes in v4:
time: 49.6 us; the launch traced here: 48.8 us
  Pallas kernels  46.8 us (94%)
  local copies, waits for them, and re-layouts  1.32 us (3%)
  between operations  0.66 us (1%)
    pallas_call x1, Pallas kernels, on_device(): pl.pallas_call(functools.partial(kernel, shards, steps), out_shape=jax.Sh...  46.8 us
    unnamed x1, local copies, waits for them, and re-layouts  1.32 us

profile of v4, /device:TPU:2, one launch (start us, length us, event | category | flops | bytes accessed | tf_op | source)
XLA Modules:
  0.0 48.8 jit_solution(3983218078374791625)
XLA Ops:
  0.7 46.8 %shard_map.46 = bf16[512,2048]{1,0:T(8,128)(2,1)S(1)} custom-call(bf16[512,2048]{1,0:T(8,128)(2,1)} %velocity.1, bf16[2048,1024]{1,0:T(8,128)(2,1)} %modes.1, s32[1,512]{1,0:T(1,128)} %bitcast.1, s32[1]{0:T(128)S(6)} %copy.6.counts), custom_call_target="tpu_custom_call" | custom-call | tf_op jit(solution)/shard_map/pallas_call | solution.py:285
  47.4 1.3 %copy.7 = bf16[512,2048]{1,0:T(8,128)(2,1)} copy(bf16[512,2048]{1,0:T(8,128)(2,1)S(1)} %shard_map.46) | data formatting | bytes 4194304
